TPU v7x, 32 devices: a whole 2x2x4 slice. The times are simulated.
32 devices in a mesh: beam: 2 (over y), fft: 4 (over z), chan: 4 (over x, core).
Axes of the slice: x: 2, y: 2, z: 4, core: 2. Of those that a mesh axis runs over, the one named last changes fastest.
Arguments:
- filterbank: bfloat16 [8192, 16384], P(('beam', 'chan'), 'fft'), parts along dimension 0, may hold values from -6 to 6
- delays: int32 [4096, 16], P('chan'), may hold values from 0 to 15, as said below
- template_bank: bfloat16 [2, 128, 32], replicated, may hold values from -1 to 1
- accel_index: int32 [64], replicated, may hold values from 0 to 127, as said below
Outputs:
- peaks: float32 [32, 64, 64], P(('beam', 'fft', 'chan')), parts along dimension 0
- energy: float32 [32], P(('beam', 'fft', 'chan')), parts along dimension 0
There are 2 independent parts, one for each index of `beam`. A program takes and returns all parts, laid end to end along the dimension named above; an argument that names none is the same for every part. Nothing has to cross between parts.
Inputs may be any that keep to these rules, and one draw needn't show every extreme that they name: `delays`: follows the cold-plasma law: proportional to the trial measure times the channel's inverse squared frequency less that of the band's top, rounded down; the trial measures rise over the whole range; non-increasing along channels and non-decreasing along trial measures; the first channel reaches 15 at the last trial measure. `accel_index`: distinct and increasing; the first is 0 and the last is 127.
All inputs are finite; a program needn't handle non-finite values.
Results may differ from a plain program's by a relative error of at most 0.0021.
Values may be sent and summed in bfloat16 or wider, within the bound.
A program may use at most 64 MiB of HBM per device.

v0:
```python
import jax
import jax.numpy as jnp
from jax import lax
from jax.sharding import PartitionSpec as P

CHAN = 4096
MAXD = 16


TWO_PI = 6.283185307179586


def from_behind(block, axis, distance):
    devices = range(lax.axis_size(axis))
    route = [(i - distance, i) for i in devices if i - distance in devices]
    return lax.ppermute(block, axis, route)


def dedisperse(columns, extended, samples):

    def accumulate(offset, running):
        picked = (columns.T == offset).astype(jnp.bfloat16)
        window = lax.dynamic_slice_in_dim(extended, offset * 128, samples, 1)
        return running + jnp.dot(picked, window, preferred_element_type=jnp.float32)

    return lax.fori_loop(0, MAXD, accumulate, jnp.zeros((columns.shape[1], samples), jnp.float32))


def spectrum(series):
    series_count, length = series.shape
    width_two = length // 128
    grid_view = series.reshape(series_count, 128, width_two)
    rows_first = lax.iota(jnp.int32, 128)
    cols_second = lax.iota(jnp.int32, width_two)
    highest = lax.Precision.HIGHEST
    first_angle = (
        TWO_PI * (rows_first[:, None] * rows_first[None, :] % 128).astype(jnp.float32) / 128.0
    )
    real_one = jnp.einsum("ka,dab->dkb", jnp.cos(first_angle), grid_view, precision=highest)
    imag_one = -jnp.einsum("ka,dab->dkb", jnp.sin(first_angle), grid_view, precision=highest)
    twiddle = (
        TWO_PI * (rows_first[:, None] * cols_second[None, :] % length).astype(jnp.float32) / length
    )
    twist_cos = jnp.cos(twiddle)
    twist_sin = jnp.sin(twiddle)
    real_two = real_one * twist_cos + imag_one * twist_sin
    imag_two = imag_one * twist_cos - real_one * twist_sin
    half_width = width_two // 2
    cols_out = lax.iota(jnp.int32, half_width)
    second_angle = (
        TWO_PI
        * (cols_second[:, None] * cols_out[None, :] % width_two).astype(jnp.float32)
        / width_two
    )
    second_cos = jnp.cos(second_angle)
    second_sin = jnp.sin(second_angle)
    real_out = jnp.einsum("dkb,bm->dkm", real_two, second_cos, precision=highest) + jnp.einsum(
        "dkb,bm->dkm", imag_two, second_sin, precision=highest
    )
    imag_out = jnp.einsum("dkb,bm->dkm", imag_two, second_cos, precision=highest) - jnp.einsum(
        "dkb,bm->dkm", real_two, second_sin, precision=highest
    )
    norm_scale = length ** (-0.5)
    real_out = real_out.transpose(0, 2, 1).reshape(series_count, length // 2) * norm_scale
    imag_out = imag_out.transpose(0, 2, 1).reshape(series_count, length // 2) * norm_scale
    return (real_out, imag_out)


def correlate(spec_real, spec_imag, kernel_stack):
    series_count, bin_total = spec_real.shape
    taps_count = kernel_stack.shape[1]
    templates = kernel_stack.shape[0] // 2
    lead_taps = taps_count // 2
    pad_real = jnp.pad(
        spec_real.astype(jnp.bfloat16), ((0, 0), (lead_taps, taps_count - lead_taps))
    )
    pad_imag = jnp.pad(
        spec_imag.astype(jnp.bfloat16), ((0, 0), (lead_taps, taps_count - lead_taps))
    )
    block_bins = bin_total // 8

    def one_block(block_index):
        seg_real = lax.dynamic_slice_in_dim(
            pad_real, block_index * block_bins, block_bins + taps_count, 1
        )
        seg_imag = lax.dynamic_slice_in_dim(
            pad_imag, block_index * block_bins, block_bins + taps_count, 1
        )
        win_real = jnp.stack(
            [seg_real[:, lag_index : lag_index + block_bins] for lag_index in range(taps_count)],
            axis=1,
        )
        win_imag = jnp.stack(
            [seg_imag[:, lag_index : lag_index + block_bins] for lag_index in range(taps_count)],
            axis=1,
        )
        from_real = jnp.einsum(
            "am,dmk->dak", kernel_stack, win_real, preferred_element_type=jnp.float32
        )
        from_imag = jnp.einsum(
            "am,dmk->dak", kernel_stack, win_imag, preferred_element_type=jnp.float32
        )
        out_real = from_real[:, :templates] - from_imag[:, templates:]
        out_imag = from_imag[:, :templates] + from_real[:, templates:]
        power = out_real * out_real + out_imag * out_imag
        return jnp.max(power.reshape(series_count, templates, block_bins // 128, 128), axis=3)

    block_peaks = lax.map(one_block, jnp.arange(8, dtype=jnp.int32))
    return block_peaks.transpose(1, 2, 0, 3).reshape(series_count, templates, bin_total // 128)


def body(filterbank, delays, template_bank, accel_index):
    channels, samples = filterbank.shape
    fft_count = lax.axis_size("fft")
    chan_count = lax.axis_size("chan")
    dm_total = delays.shape[1]
    rim_width = MAXD * 128
    columns = delays.reshape(channels, fft_count, chan_count, dm_total // (fft_count * chan_count))
    columns = columns.transpose(0, 2, 1, 3).reshape(channels, dm_total)
    carried = None
    blank = jnp.zeros((channels, rim_width), jnp.bfloat16)
    extended = jnp.concatenate([filterbank, blank], axis=1)
    before = jnp.concatenate([blank, filterbank[:, :rim_width]], axis=1)
    carried = from_behind(dedisperse(columns, before, rim_width), "fft", -1)
    partial_value = dedisperse(columns, extended, samples)
    partial_value = jnp.concatenate(
        [
            partial_value[:, : samples - rim_width],
            partial_value[:, samples - rim_width :] + carried,
        ],
        axis=1,
    )
    reduced = lax.psum_scatter(partial_value, "chan", scatter_dimension=0, tiled=True)
    series = lax.all_to_all(reduced, "fft", split_axis=0, concat_axis=1, tiled=True)
    series = series * CHAN ** (-0.5)
    spec_real, spec_imag = spectrum(series)
    bank_size = template_bank.shape[1]
    selector = (accel_index[:, None] == lax.iota(jnp.int32, bank_size)[None, :]).astype(
        jnp.bfloat16
    )
    kernel_real = jnp.dot(selector, template_bank[0], preferred_element_type=jnp.float32)
    kernel_imag = jnp.dot(selector, template_bank[1], preferred_element_type=jnp.float32)
    kernel_stack = jnp.concatenate([kernel_real, kernel_imag], axis=0).astype(jnp.bfloat16)
    peaks = correlate(spec_real, spec_imag, kernel_stack)
    energy = jnp.sum(spec_real * spec_real + spec_imag * spec_imag, axis=1)
    return (peaks, energy)


def solution(mesh):
    in_specs = (P(("beam", "chan"), "fft"), P("chan", None), P(), P())
    out_specs = (P(("beam", "fft", "chan"), None, None), P(("beam", "fft", "chan")))
    return jax.shard_map(body, mesh=mesh, in_specs=in_specs, out_specs=out_specs, check_vma=False)
```

profile of v0, /device:TPU:0, one launch (start us, length us, event | category | flops | bytes accessed | tf_op | source)
XLA Modules:
  0.0 239.2 jit_solution(6277641440804771692)
XLA Ops:
  7.2 0.9 reshape.189
  8.2 4.7 %slice.221 = bf16[1024,2048]{1,0:T(8,128)(2,1)} slice(bf16[1024,4096]{1,0:T(8,128)(2,1)} %param.10), slice={[0:1024], [0:2048]} | slice | bytes 8388608 | tf_op jit(solution)/shard_map/slice | solution.py:123
  12.9 6.6 %concatenate.14 = bf16[1024,4096]{1,0:T(8,128)(2,1)} pad(bf16[1024,2048]{1,0:T(8,128)(2,1)} %slice.221, bf16[]{:T(256)} %constant.122.clone.1), padding=0_0x2048_0 | pad | bytes 12582914 | tf_op jit(solution)/shard_map/concatenate | solution.py:123
  19.5 45.6 %while.40 = (s32[]{:T(128)}, f32[16,2048]{1,0:T(8,128)S(1)}, s32[1024,16]{0,1:T(8,128)S(1)}, bf16[1024,4096]{1,0:T(8,128)(2,1)}, s32[]{:T(128)}, /*index=5*/s32[]{:T(128)}, s32[]{:T(128)}, s32[]{:T(128)}) while((s32[]{:T(128)}, f32[16,2048]{1,0:T(8,128)S(1)}, s32[1024,16]{0,1:T(8,128)S(1)}, bf16[1024,4096]{1,0:T(8,128)(2,1)}, ...), condition=%wide.region_3.0_spmd.clone, body=%wide.region_2.0_spmd.clone.sunk | while | flops 67190792 | bytes 4522641 | solution.py:26
  19.5 2.8 %fusion.203 = f32[16,2048]{1,0:T(8,128)S(1)} fusion(bf16[1024,4096]{1,0:T(8,128)(2,1)} %get-tuple-element.618, s32[]{:T(128)S(6)} %select_n.127, f32[16,2048]{1,0:T(8,128)S(1)} %get-tuple-element.608, pred[]{:T(512)S(6)} %compare.23, s32[1024,16]{0,1:T(8,128)S(1)} %get-tuple-element.617, s32[]{:T(128)} %get-tuple-element.607), kind=kOutput, calls=%fused_computation.147.clone.1 | convolution fusion | flops 67190784 | bytes 4522501 | tf_op jit(solution)/shard_map/while/body/eval_jaxpr/dot_general | solution.py:24
  22.3 2.8 %fusion.203 = f32[16,2048]{1,0:T(8,128)S(1)} fusion(bf16[1024,4096]{1,0:T(8,128)(2,1)} %get-tuple-element.618, s32[]{:T(128)S(6)} %select_n.127, f32[16,2048]{1,0:T(8,128)S(1)} %get-tuple-element.608, pred[]{:T(512)S(6)} %compare.23, s32[1024,16]{0,1:T(8,128)S(1)} %get-tuple-element.617, s32[]{:T(128)} %get-tuple-element.607), kind=kOutput, calls=%fused_computation.147.clone.1 | convolution fusion | flops 67190784 | bytes 4522501 | tf_op jit(solution)/shard_map/while/body/eval_jaxpr/dot_general | solution.py:24
  25.2 2.8 %fusion.203 = f32[16,2048]{1,0:T(8,128)S(1)} fusion(bf16[1024,4096]{1,0:T(8,128)(2,1)} %get-tuple-element.618, s32[]{:T(128)S(6)} %select_n.127, f32[16,2048]{1,0:T(8,128)S(1)} %get-tuple-element.608, pred[]{:T(512)S(6)} %compare.23, s32[1024,16]{0,1:T(8,128)S(1)} %get-tuple-element.617, s32[]{:T(128)} %get-tuple-element.607), kind=kOutput, calls=%fused_computation.147.clone.1 | convolution fusion | flops 67190784 | bytes 4522501 | tf_op jit(solution)/shard_map/while/body/eval_jaxpr/dot_general | solution.py:24
  28.0 2.8 %fusion.203 = f32[16,2048]{1,0:T(8,128)S(1)} fusion(bf16[1024,4096]{1,0:T(8,128)(2,1)} %get-tuple-element.618, s32[]{:T(128)S(6)} %select_n.127, f32[16,2048]{1,0:T(8,128)S(1)} %get-tuple-element.608, pred[]{:T(512)S(6)} %compare.23, s32[1024,16]{0,1:T(8,128)S(1)} %get-tuple-element.617, s32[]{:T(128)} %get-tuple-element.607), kind=kOutput, calls=%fused_computation.147.clone.1 | convolution fusion | flops 67190784 | bytes 4522501 | tf_op jit(solution)/shard_map/while/body/eval_jaxpr/dot_general | solution.py:24
  30.9 2.8 %fusion.203 = f32[16,2048]{1,0:T(8,128)S(1)} fusion(bf16[1024,4096]{1,0:T(8,128)(2,1)} %get-tuple-element.618, s32[]{:T(128)S(6)} %select_n.127, f32[16,2048]{1,0:T(8,128)S(1)} %get-tuple-element.608, pred[]{:T(512)S(6)} %compare.23, s32[1024,16]{0,1:T(8,128)S(1)} %get-tuple-element.617, s32[]{:T(128)} %get-tuple-element.607), kind=kOutput, calls=%fused_computation.147.clone.1 | convolution fusion | flops 67190784 | bytes 4522501 | tf_op jit(solution)/shard_map/while/body/eval_jaxpr/dot_general | solution.py:24
  33.7 2.8 %fusion.203 = f32[16,2048]{1,0:T(8,128)S(1)} fusion(bf16[1024,4096]{1,0:T(8,128)(2,1)} %get-tuple-element.618, s32[]{:T(128)S(6)} %select_n.127, f32[16,2048]{1,0:T(8,128)S(1)} %get-tuple-element.608, pred[]{:T(512)S(6)} %compare.23, s32[1024,16]{0,1:T(8,128)S(1)} %get-tuple-element.617, s32[]{:T(128)} %get-tuple-element.607), kind=kOutput, calls=%fused_computation.147.clone.1 | convolution fusion | flops 67190784 | bytes 4522501 | tf_op jit(solution)/shard_map/while/body/eval_jaxpr/dot_general | solution.py:24
  36.6 2.8 %fusion.203 = f32[16,2048]{1,0:T(8,128)S(1)} fusion(bf16[1024,4096]{1,0:T(8,128)(2,1)} %get-tuple-element.618, s32[]{:T(128)S(6)} %select_n.127, f32[16,2048]{1,0:T(8,128)S(1)} %get-tuple-element.608, pred[]{:T(512)S(6)} %compare.23, s32[1024,16]{0,1:T(8,128)S(1)} %get-tuple-element.617, s32[]{:T(128)} %get-tuple-element.607), kind=kOutput, calls=%fused_computation.147.clone.1 | convolution fusion | flops 67190784 | bytes 4522501 | tf_op jit(solution)/shard_map/while/body/eval_jaxpr/dot_general | solution.py:24
  39.4 2.8 %fusion.203 = f32[16,2048]{1,0:T(8,128)S(1)} fusion(bf16[1024,4096]{1,0:T(8,128)(2,1)} %get-tuple-element.618, s32[]{:T(128)S(6)} %select_n.127, f32[16,2048]{1,0:T(8,128)S(1)} %get-tuple-element.608, pred[]{:T(512)S(6)} %compare.23, s32[1024,16]{0,1:T(8,128)S(1)} %get-tuple-element.617, s32[]{:T(128)} %get-tuple-element.607), kind=kOutput, calls=%fused_computation.147.clone.1 | convolution fusion | flops 67190784 | bytes 4522501 | tf_op jit(solution)/shard_map/while/body/eval_jaxpr/dot_general | solution.py:24
  42.3 2.8 %fusion.203 = f32[16,2048]{1,0:T(8,128)S(1)} fusion(bf16[1024,4096]{1,0:T(8,128)(2,1)} %get-tuple-element.618, s32[]{:T(128)S(6)} %select_n.127, f32[16,2048]{1,0:T(8,128)S(1)} %get-tuple-element.608, pred[]{:T(512)S(6)} %compare.23, s32[1024,16]{0,1:T(8,128)S(1)} %get-tuple-element.617, s32[]{:T(128)} %get-tuple-element.607), kind=kOutput, calls=%fused_computation.147.clone.1 | convolution fusion | flops 67190784 | bytes 4522501 | tf_op jit(solution)/shard_map/while/body/eval_jaxpr/dot_general | solution.py:24
  45.1 2.8 %fusion.203 = f32[16,2048]{1,0:T(8,128)S(1)} fusion(bf16[1024,4096]{1,0:T(8,128)(2,1)} %get-tuple-element.618, s32[]{:T(128)S(6)} %select_n.127, f32[16,2048]{1,0:T(8,128)S(1)} %get-tuple-element.608, pred[]{:T(512)S(6)} %compare.23, s32[1024,16]{0,1:T(8,128)S(1)} %get-tuple-element.617, s32[]{:T(128)} %get-tuple-element.607), kind=kOutput, calls=%fused_computation.147.clone.1 | convolution fusion | flops 67190784 | bytes 4522501 | tf_op jit(solution)/shard_map/while/body/eval_jaxpr/dot_general | solution.py:24
  48.0 2.8 %fusion.203 = f32[16,2048]{1,0:T(8,128)S(1)} fusion(bf16[1024,4096]{1,0:T(8,128)(2,1)} %get-tuple-element.618, s32[]{:T(128)S(6)} %select_n.127, f32[16,2048]{1,0:T(8,128)S(1)} %get-tuple-element.608, pred[]{:T(512)S(6)} %compare.23, s32[1024,16]{0,1:T(8,128)S(1)} %get-tuple-element.617, s32[]{:T(128)} %get-tuple-element.607), kind=kOutput, calls=%fused_computation.147.clone.1 | convolution fusion | flops 67190784 | bytes 4522501 | tf_op jit(solution)/shard_map/while/body/eval_jaxpr/dot_general | solution.py:24
  50.8 2.8 %fusion.203 = f32[16,2048]{1,0:T(8,128)S(1)} fusion(bf16[1024,4096]{1,0:T(8,128)(2,1)} %get-tuple-element.618, s32[]{:T(128)S(6)} %select_n.127, f32[16,2048]{1,0:T(8,128)S(1)} %get-tuple-element.608, pred[]{:T(512)S(6)} %compare.23, s32[1024,16]{0,1:T(8,128)S(1)} %get-tuple-element.617, s32[]{:T(128)} %get-tuple-element.607), kind=kOutput, calls=%fused_computation.147.clone.1 | convolution fusion | flops 67190784 | bytes 4522501 | tf_op jit(solution)/shard_map/while/body/eval_jaxpr/dot_general | solution.py:24
  53.7 2.8 %fusion.203 = f32[16,2048]{1,0:T(8,128)S(1)} fusion(bf16[1024,4096]{1,0:T(8,128)(2,1)} %get-tuple-element.618, s32[]{:T(128)S(6)} %select_n.127, f32[16,2048]{1,0:T(8,128)S(1)} %get-tuple-element.608, pred[]{:T(512)S(6)} %compare.23, s32[1024,16]{0,1:T(8,128)S(1)} %get-tuple-element.617, s32[]{:T(128)} %get-tuple-element.607), kind=kOutput, calls=%fused_computation.147.clone.1 | convolution fusion | flops 67190784 | bytes 4522501 | tf_op jit(solution)/shard_map/while/body/eval_jaxpr/dot_general | solution.py:24
  56.5 2.8 %fusion.203 = f32[16,2048]{1,0:T(8,128)S(1)} fusion(bf16[1024,4096]{1,0:T(8,128)(2,1)} %get-tuple-element.618, s32[]{:T(128)S(6)} %select_n.127, f32[16,2048]{1,0:T(8,128)S(1)} %get-tuple-element.608, pred[]{:T(512)S(6)} %compare.23, s32[1024,16]{0,1:T(8,128)S(1)} %get-tuple-element.617, s32[]{:T(128)} %get-tuple-element.607), kind=kOutput, calls=%fused_computation.147.clone.1 | convolution fusion | flops 67190784 | bytes 4522501 | tf_op jit(solution)/shard_map/while/body/eval_jaxpr/dot_general | solution.py:24
  59.4 2.8 %fusion.203 = f32[16,2048]{1,0:T(8,128)S(1)} fusion(bf16[1024,4096]{1,0:T(8,128)(2,1)} %get-tuple-element.618, s32[]{:T(128)S(6)} %select_n.127, f32[16,2048]{1,0:T(8,128)S(1)} %get-tuple-element.608, pred[]{:T(512)S(6)} %compare.23, s32[1024,16]{0,1:T(8,128)S(1)} %get-tuple-element.617, s32[]{:T(128)} %get-tuple-element.607), kind=kOutput, calls=%fused_computation.147.clone.1 | convolution fusion | flops 67190784 | bytes 4522501 | tf_op jit(solution)/shard_map/while/body/eval_jaxpr/dot_general | solution.py:24
  62.2 2.8 %fusion.203 = f32[16,2048]{1,0:T(8,128)S(1)} fusion(bf16[1024,4096]{1,0:T(8,128)(2,1)} %get-tuple-element.618, s32[]{:T(128)S(6)} %select_n.127, f32[16,2048]{1,0:T(8,128)S(1)} %get-tuple-element.608, pred[]{:T(512)S(6)} %compare.23, s32[1024,16]{0,1:T(8,128)S(1)} %get-tuple-element.617, s32[]{:T(128)} %get-tuple-element.607), kind=kOutput, calls=%fused_computation.147.clone.1 | convolution fusion | flops 67190784 | bytes 4522501 | tf_op jit(solution)/shard_map/while/body/eval_jaxpr/dot_general | solution.py:24
  65.1 1.3 collective-permute-start
  66.4 9.2 %concatenate.13 = bf16[1024,6144]{1,0:T(8,128)(2,1)} pad(bf16[1024,4096]{1,0:T(8,128)(2,1)} %param.10, bf16[]{:T(256)} %constant.122.clone.1), padding=0_0x0_2048 | pad | bytes 20971522 | tf_op jit(solution)/shard_map/concatenate | solution.py:122
  75.5 73.4 %while.39 = (s32[]{:T(128)}, f32[16,4096]{1,0:T(8,128)S(1)}, s32[1024,16]{0,1:T(8,128)S(1)}, bf16[1024,6144]{1,0:T(8,128)(2,1)}, s32[]{:T(128)}, /*index=5*/s32[]{:T(128)}, s32[]{:T(128)}, s32[]{:T(128)}) while((s32[]{:T(128)}, f32[16,4096]{1,0:T(8,128)S(1)}, s32[1024,16]{0,1:T(8,128)S(1)}, bf16[1024,6144]{1,0:T(8,128)(2,1)}, ...), condition=%wide.region_1.0_spmd.clone, body=%wide.region_0.0_spmd.clone.sunk | while | flops 134365184 | bytes 8979089 | solution.py:26
  75.5 4.6 %fusion.200 = f32[16,4096]{1,0:T(8,128)S(1)} fusion(bf16[1024,6144]{1,0:T(8,128)(2,1)} %get-tuple-element.594, s32[]{:T(128)S(6)} %select_n.126, f32[16,4096]{1,0:T(8,128)S(1)} %get-tuple-element.584, pred[]{:T(512)S(6)} %compare.22, s32[1024,16]{0,1:T(8,128)S(1)} %get-tuple-element.593, s32[]{:T(128)} %get-tuple-element.583), kind=kOutput, calls=%fused_computation.141.clone.1 | convolution fusion | flops 134365184 | bytes 8978949 | tf_op jit(solution)/shard_map/while/body/eval_jaxpr/dot_general | solution.py:24
  80.1 4.6 %fusion.200 = f32[16,4096]{1,0:T(8,128)S(1)} fusion(bf16[1024,6144]{1,0:T(8,128)(2,1)} %get-tuple-element.594, s32[]{:T(128)S(6)} %select_n.126, f32[16,4096]{1,0:T(8,128)S(1)} %get-tuple-element.584, pred[]{:T(512)S(6)} %compare.22, s32[1024,16]{0,1:T(8,128)S(1)} %get-tuple-element.593, s32[]{:T(128)} %get-tuple-element.583), kind=kOutput, calls=%fused_computation.141.clone.1 | convolution fusion | flops 134365184 | bytes 8978949 | tf_op jit(solution)/shard_map/while/body/eval_jaxpr/dot_general | solution.py:24
  84.7 4.6 %fusion.200 = f32[16,4096]{1,0:T(8,128)S(1)} fusion(bf16[1024,6144]{1,0:T(8,128)(2,1)} %get-tuple-element.594, s32[]{:T(128)S(6)} %select_n.126, f32[16,4096]{1,0:T(8,128)S(1)} %get-tuple-element.584, pred[]{:T(512)S(6)} %compare.22, s32[1024,16]{0,1:T(8,128)S(1)} %get-tuple-element.593, s32[]{:T(128)} %get-tuple-element.583), kind=kOutput, calls=%fused_computation.141.clone.1 | convolution fusion | flops 134365184 | bytes 8978949 | tf_op jit(solution)/shard_map/while/body/eval_jaxpr/dot_general | solution.py:24
  89.3 4.6 %fusion.200 = f32[16,4096]{1,0:T(8,128)S(1)} fusion(bf16[1024,6144]{1,0:T(8,128)(2,1)} %get-tuple-element.594, s32[]{:T(128)S(6)} %select_n.126, f32[16,4096]{1,0:T(8,128)S(1)} %get-tuple-element.584, pred[]{:T(512)S(6)} %compare.22, s32[1024,16]{0,1:T(8,128)S(1)} %get-tuple-element.593, s32[]{:T(128)} %get-tuple-element.583), kind=kOutput, calls=%fused_computation.141.clone.1 | convolution fusion | flops 134365184 | bytes 8978949 | tf_op jit(solution)/shard_map/while/body/eval_jaxpr/dot_general | solution.py:24
  93.9 4.6 %fusion.200 = f32[16,4096]{1,0:T(8,128)S(1)} fusion(bf16[1024,6144]{1,0:T(8,128)(2,1)} %get-tuple-element.594, s32[]{:T(128)S(6)} %select_n.126, f32[16,4096]{1,0:T(8,128)S(1)} %get-tuple-element.584, pred[]{:T(512)S(6)} %compare.22, s32[1024,16]{0,1:T(8,128)S(1)} %get-tuple-element.593, s32[]{:T(128)} %get-tuple-element.583), kind=kOutput, calls=%fused_computation.141.clone.1 | convolution fusion | flops 134365184 | bytes 8978949 | tf_op jit(solution)/shard_map/while/body/eval_jaxpr/dot_general | solution.py:24
  98.5 4.6 %fusion.200 = f32[16,4096]{1,0:T(8,128)S(1)} fusion(bf16[1024,6144]{1,0:T(8,128)(2,1)} %get-tuple-element.594, s32[]{:T(128)S(6)} %select_n.126, f32[16,4096]{1,0:T(8,128)S(1)} %get-tuple-element.584, pred[]{:T(512)S(6)} %compare.22, s32[1024,16]{0,1:T(8,128)S(1)} %get-tuple-element.593, s32[]{:T(128)} %get-tuple-element.583), kind=kOutput, calls=%fused_computation.141.clone.1 | convolution fusion | flops 134365184 | bytes 8978949 | tf_op jit(solution)/shard_map/while/body/eval_jaxpr/dot_general | solution.py:24
  103.0 4.6 %fusion.200 = f32[16,4096]{1,0:T(8,128)S(1)} fusion(bf16[1024,6144]{1,0:T(8,128)(2,1)} %get-tuple-element.594, s32[]{:T(128)S(6)} %select_n.126, f32[16,4096]{1,0:T(8,128)S(1)} %get-tuple-element.584, pred[]{:T(512)S(6)} %compare.22, s32[1024,16]{0,1:T(8,128)S(1)} %get-tuple-element.593, s32[]{:T(128)} %get-tuple-element.583), kind=kOutput, calls=%fused_computation.141.clone.1 | convolution fusion | flops 134365184 | bytes 8978949 | tf_op jit(solution)/shard_map/while/body/eval_jaxpr/dot_general | solution.py:24
  107.6 4.6 %fusion.200 = f32[16,4096]{1,0:T(8,128)S(1)} fusion(bf16[1024,6144]{1,0:T(8,128)(2,1)} %get-tuple-element.594, s32[]{:T(128)S(6)} %select_n.126, f32[16,4096]{1,0:T(8,128)S(1)} %get-tuple-element.584, pred[]{:T(512)S(6)} %compare.22, s32[1024,16]{0,1:T(8,128)S(1)} %get-tuple-element.593, s32[]{:T(128)} %get-tuple-element.583), kind=kOutput, calls=%fused_computation.141.clone.1 | convolution fusion | flops 134365184 | bytes 8978949 | tf_op jit(solution)/shard_map/while/body/eval_jaxpr/dot_general | solution.py:24
  112.2 4.6 %fusion.200 = f32[16,4096]{1,0:T(8,128)S(1)} fusion(bf16[1024,6144]{1,0:T(8,128)(2,1)} %get-tuple-element.594, s32[]{:T(128)S(6)} %select_n.126, f32[16,4096]{1,0:T(8,128)S(1)} %get-tuple-element.584, pred[]{:T(512)S(6)} %compare.22, s32[1024,16]{0,1:T(8,128)S(1)} %get-tuple-element.593, s32[]{:T(128)} %get-tuple-element.583), kind=kOutput, calls=%fused_computation.141.clone.1 | convolution fusion | flops 134365184 | bytes 8978949 | tf_op jit(solution)/shard_map/while/body/eval_jaxpr/dot_general | solution.py:24
  116.8 4.6 %fusion.200 = f32[16,4096]{1,0:T(8,128)S(1)} fusion(bf16[1024,6144]{1,0:T(8,128)(2,1)} %get-tuple-element.594, s32[]{:T(128)S(6)} %select_n.126, f32[16,4096]{1,0:T(8,128)S(1)} %get-tuple-element.584, pred[]{:T(512)S(6)} %compare.22, s32[1024,16]{0,1:T(8,128)S(1)} %get-tuple-element.593, s32[]{:T(128)} %get-tuple-element.583), kind=kOutput, calls=%fused_computation.141.clone.1 | convolution fusion | flops 134365184 | bytes 8978949 | tf_op jit(solution)/shard_map/while/body/eval_jaxpr/dot_general | solution.py:24
  121.4 4.6 %fusion.200 = f32[16,4096]{1,0:T(8,128)S(1)} fusion(bf16[1024,6144]{1,0:T(8,128)(2,1)} %get-tuple-element.594, s32[]{:T(128)S(6)} %select_n.126, f32[16,4096]{1,0:T(8,128)S(1)} %get-tuple-element.584, pred[]{:T(512)S(6)} %compare.22, s32[1024,16]{0,1:T(8,128)S(1)} %get-tuple-element.593, s32[]{:T(128)} %get-tuple-element.583), kind=kOutput, calls=%fused_computation.141.clone.1 | convolution fusion | flops 134365184 | bytes 8978949 | tf_op jit(solution)/shard_map/while/body/eval_jaxpr/dot_general | solution.py:24
  126.0 4.6 %fusion.200 = f32[16,4096]{1,0:T(8,128)S(1)} fusion(bf16[1024,6144]{1,0:T(8,128)(2,1)} %get-tuple-element.594, s32[]{:T(128)S(6)} %select_n.126, f32[16,4096]{1,0:T(8,128)S(1)} %get-tuple-element.584, pred[]{:T(512)S(6)} %compare.22, s32[1024,16]{0,1:T(8,128)S(1)} %get-tuple-element.593, s32[]{:T(128)} %get-tuple-element.583), kind=kOutput, calls=%fused_computation.141.clone.1 | convolution fusion | flops 134365184 | bytes 8978949 | tf_op jit(solution)/shard_map/while/body/eval_jaxpr/dot_general | solution.py:24
  130.6 4.6 %fusion.200 = f32[16,4096]{1,0:T(8,128)S(1)} fusion(bf16[1024,6144]{1,0:T(8,128)(2,1)} %get-tuple-element.594, s32[]{:T(128)S(6)} %select_n.126, f32[16,4096]{1,0:T(8,128)S(1)} %get-tuple-element.584, pred[]{:T(512)S(6)} %compare.22, s32[1024,16]{0,1:T(8,128)S(1)} %get-tuple-element.593, s32[]{:T(128)} %get-tuple-element.583), kind=kOutput, calls=%fused_computation.141.clone.1 | convolution fusion | flops 134365184 | bytes 8978949 | tf_op jit(solution)/shard_map/while/body/eval_jaxpr/dot_general | solution.py:24
  135.2 4.6 %fusion.200 = f32[16,4096]{1,0:T(8,128)S(1)} fusion(bf16[1024,6144]{1,0:T(8,128)(2,1)} %get-tuple-element.594, s32[]{:T(128)S(6)} %select_n.126, f32[16,4096]{1,0:T(8,128)S(1)} %get-tuple-element.584, pred[]{:T(512)S(6)} %compare.22, s32[1024,16]{0,1:T(8,128)S(1)} %get-tuple-element.593, s32[]{:T(128)} %get-tuple-element.583), kind=kOutput, calls=%fused_computation.141.clone.1 | convolution fusion | flops 134365184 | bytes 8978949 | tf_op jit(solution)/shard_map/while/body/eval_jaxpr/dot_general | solution.py:24
  139.8 4.6 %fusion.200 = f32[16,4096]{1,0:T(8,128)S(1)} fusion(bf16[1024,6144]{1,0:T(8,128)(2,1)} %get-tuple-element.594, s32[]{:T(128)S(6)} %select_n.126, f32[16,4096]{1,0:T(8,128)S(1)} %get-tuple-element.584, pred[]{:T(512)S(6)} %compare.22, s32[1024,16]{0,1:T(8,128)S(1)} %get-tuple-element.593, s32[]{:T(128)} %get-tuple-element.583), kind=kOutput, calls=%fused_computation.141.clone.1 | convolution fusion | flops 134365184 | bytes 8978949 | tf_op jit(solution)/shard_map/while/body/eval_jaxpr/dot_general | solution.py:24
  144.3 4.6 %fusion.200 = f32[16,4096]{1,0:T(8,128)S(1)} fusion(bf16[1024,6144]{1,0:T(8,128)(2,1)} %get-tuple-element.594, s32[]{:T(128)S(6)} %select_n.126, f32[16,4096]{1,0:T(8,128)S(1)} %get-tuple-element.584, pred[]{:T(512)S(6)} %compare.22, s32[1024,16]{0,1:T(8,128)S(1)} %get-tuple-element.593, s32[]{:T(128)} %get-tuple-element.583), kind=kOutput, calls=%fused_computation.141.clone.1 | convolution fusion | flops 134365184 | bytes 8978949 | tf_op jit(solution)/shard_map/while/body/eval_jaxpr/dot_general | solution.py:24
  150.4 0.7 pad_maximum_fusion
  151.4 36.0 %all-reduce.7.cloned.1.call-done = f32[16,4096]{1,0:T(8,128)} async-done(((f32[16,4096]{1,0:T(8,128)}), f32[16,4096]{1,0:T(8,128)}) %all-reduce.7.cloned.1.call-update) | async-done | bytes 262160
  187.4 0.9 dynamic-slice_bitcast_fusion
  189.0 4.6 %all-to-all-start = ((f32[4,1,4096]{2,1,0:T(1,128)}), f32[4,1,4096]{2,1,0:T(1,128)S(1)}, u32[]{:S(2)}, u32[]{:S(2)}) async-start(f32[4,1,4096]{2,1,0:T(1,128)} %copy.14), calls=%async_computation | async-start | bytes 131072 | tf_op jit(solution)/shard_map/all_to_all | solution.py:134
  193.8 5.5 %all-to-all-done = f32[4,1,4096]{2,1,0:T(1,128)S(1)} async-done(((f32[4,1,4096]{2,1,0:T(1,128)}), f32[4,1,4096]{2,1,0:T(1,128)S(1)}, u32[]{:S(2)}, u32[]{:S(2)}) %all-to-all-start) | async-done | bytes 65568 | tf_op jit(solution)/shard_map/all_to_all | solution.py:134
  201.8 0.7 fusion.87
  202.5 1.3 add_reduce_fusion
  204.1 27.5 %while.38 = (s32[]{:T(128)}, f32[8,1,64,8]{2,3,0,1:T(8,128)S(1)}, s32[8]{0:T(128)S(1)}, bf16[1,8224]{1,0:T(2,128)(2,1)S(1)}, bf16[128,32]{1,0:T(8,128)(2,1)S(1)}...) while((s32[]{:T(128)}, f32[8,1,64,8]{2,3,0,1:T(8,128)S(1)}, ...), condition=%wide.region_7.8_spmd, body=%wide.region_5.7_spmd.sunk | while | flops 17169956 | bytes 3832803 | solution.py:108
  231.6 0.7 copy.17
  (134 shorter events, 26.7 us)
Async XLA Ops:
  7.2 180.2 %all-reduce.7.cloned.1.call-start = ((), (), s32[]{:S(2)}) async-start(), calls=%async_computation.1 | async-start | bytes 524288
  65.1 85.3 %collective-permute-start = (f32[16,2048]{1,0:T(8,128)S(1)}, f32[16,2048]{1,0:T(8,128)S(1)}, u32[]{:S(2)}, u32[]{:S(2)}) collective-permute-start(f32[16,2048]{1,0:T(8,128)S(1)} %get-tuple-element.193), channel_id=1, source_target_pairs={{4,0},{8,4},{12,8},{5,1},{9,5},{13,9},{6,2},{10,6},{14,10},{7,3},{... | collective-permute-start | bytes 393224 | tf_op jit(solution)/shard_map/ppermute | solution.py:16
  75.5 73.4 %copy-start.2 = (u32[32]{0:T(128)S(1)}, u32[32]{0:T(128)}, u32[]{:S(2)}) copy-start(u32[32]{0:T(128)} %constant.141) | copy-start | bytes 388
  75.5 74.7 %copy-start = (bf16[2,128,32]{1,2,0:T(8,128)(2,1)S(1)}, bf16[2,128,32]{1,2,0:T(8,128)(2,1)}, u32[]{:S(2)}) copy-start(bf16[2,128,32]{1,2,0:T(8,128)(2,1)} %param.12) | copy-start | bytes 49156
  75.5 74.7 %copy-start.1 = (s32[64]{0:T(128)S(1)}, s32[64]{0:T(128)}, u32[]{:S(2)}) copy-start(s32[64]{0:T(128)} %param.13) | copy-start | bytes 772
  189.0 10.3 %all-to-all-start = ((f32[4,1,4096]{2,1,0:T(1,128)}), f32[4,1,4096]{2,1,0:T(1,128)S(1)}, u32[]{:S(2)}, u32[]{:S(2)}) async-start(f32[4,1,4096]{2,1,0:T(1,128)} %copy.14), calls=%async_computation | async-start | bytes 131072 | tf_op jit(solution)/shard_map/all_to_all | solution.py:134
Sparse Core Ops, SparseCore 0:
  151.3 36.0 all-reduce.6
where the time goes:
time: 241 us; the launch traced here: 239 us
  matrix products  127 us (53%)
  local copies, waits for them, and re-layouts  41.7 us (17%)
  waiting for transfers between devices  41.6 us (17%)
  between operations  14.8 us (6%)
  starting transfers between devices  5.92 us (2%)
  loops' own time  5.59 us (2%)
  other arithmetic  2.68 us (1%)
    dot_general x32, matrix products, accumulate(): return running + jnp.dot(picked, window, preferred_element_type=jnp.float32)  119 us
    unnamed x2, waiting for transfers between devices  36 us
    concatenate x1, local copies, waits for them, and re-layouts, body(): extended = jnp.concatenate([filterbank, blank], axis=1)  9.16 us
    another operation x24, local copies, waits for them, and re-layouts, one_block(): jnp.stack([seg_real[:, lag_index:lag_index + block_bins] for lag_index in...  6.72 us
    concatenate x1, local copies, waits for them, and re-layouts, body(): before = jnp.concatenate([blank, filterbank[:, :rim_width]], axis=1)  6.57 us
    another operation x1, loops' own time, correlate(): block_peaks = lax.map(one_block, jnp.arange(8, dtype=jnp.int32))  5.56 us
    all_to_all x1, waiting for transfers between devices, body(): lax.all_to_all(reduced, 'fft', split_axis=0, concat_axis=1, tiled=True)  5.54 us
    dynamic_slice x8, local copies, waits for them, and re-layouts, correlate(): block_peaks = lax.map(one_block, jnp.arange(8, dtype=jnp.int32))  5.15 us
  transfers between devices with their start and end apart: 3, of which 2 were waited for; matrix products, arithmetic and copies ran while one was open for 35% of the time, Pallas kernels for 0%

commit v1 on v0

v1 whole, which is shorter than its diff:
```python
import functools

import jax
import jax.numpy as jnp
import numpy as np
from jax import lax
from jax.experimental import pallas as pl
from jax.experimental.pallas import tpu as pltpu
from jax.sharding import PartitionSpec as P

MAXD = 16
LANES = 128
MESH = pl.DeviceIdType.MESH
HIGHEST = lax.Precision.HIGHEST


def tables(length, channels_total):
    wide = length // LANES
    half = wide // 2
    rows = np.arange(LANES)
    cols = np.arange(wide)
    outs = np.arange(half)
    first = 2 * np.pi * (rows[:, None] * rows[None, :] % LANES) / LANES
    one = np.concatenate([np.cos(first), -np.sin(first)], axis=0)
    turn = 2 * np.pi * (rows[:, None] * cols[None, :] % length) / length
    scale = channels_total ** -0.5 * length ** -0.5
    twist = np.stack([np.cos(turn), np.sin(turn)]) * scale
    second = 2 * np.pi * (cols[:, None] * outs[None, :] % wide) / wide
    c2, s2 = np.cos(second), np.sin(second)
    real = np.concatenate([c2, s2], axis=0)
    imag = np.concatenate([-s2, c2], axis=0)
    two = np.concatenate([real, real, imag, imag], axis=1)
    return [jnp.asarray(t, jnp.float32) for t in (one, twist, two)]


def kernel(
    sizes,
    fb_ref, delay_ref, bank_ref, accel_ref, one_ref, twist_ref, two_ref,
    peaks_ref, energy_ref,
    xbuf, picked, acc, part, r1, q, r2, total, r3, grid_ref, tmat,
    fsem, s1, v1, s2, v2, s3, v3,
):
    fft, xs, cores, dms, blocks, chunk = sizes
    chan = xs * cores
    span = blocks + MAXD
    f = lax.axis_index("fft")
    c = lax.axis_index("chan")
    x, core = c // cores, c % cores
    columns = fb_ref.shape[1]
    chunks = columns // chunk

    def fetch(i):
        start = pl.multiple_of(i * chunk, chunk)
        return pltpu.make_async_copy(
            fb_ref.at[:, pl.ds(start, chunk)], xbuf.at[i], fsem.at[i]
        )

    for i in range(chunks):
        fetch(i).start()

    barrier = pltpu.get_barrier_semaphore()
    for k in range(1, cores):
        pl.semaphore_signal(
            barrier, inc=1, device_id={"chan": x * cores + (core + k) % cores}, device_id_type=MESH
        )
    for k in range(1, xs):
        pl.semaphore_signal(
            barrier, inc=1, device_id={"chan": ((x + k) % xs) * cores + core}, device_id_type=MESH
        )
    for k in range(1, fft):
        pl.semaphore_signal(barrier, inc=1, device_id={"fft": (f + k) % fft}, device_id_type=MESH)

    lag = delay_ref[...]
    for o in range(MAXD):
        picked[(MAXD - 1 - o) * dms:(MAXD - o) * dms, :] = jnp.where(lag == o, 1.0, 0.0).astype(
            jnp.bfloat16
        )
    acc[...] = jnp.zeros_like(acc)

    def gather_columns(i, carry):
        fetch(i).wait()
        for b in range(chunk // 256):
            y = jnp.dot(
                picked[...], xbuf[i, :, b * 256:(b + 1) * 256], preferred_element_type=jnp.float32
            )
            for h in range(2):
                row = pl.multiple_of((i * (chunk // LANES) + 2 * b + h + 1) * dms, dms)
                acc[pl.ds(row, MAXD * dms), :] += y[:, h * LANES:(h + 1) * LANES]
        return carry

    lax.fori_loop(0, chunks, gather_columns, 0)

    for k in range(cores):
        for s in range(xs):
            for g in range(fft):
                d = g * chan + s * cores + k
                part[k, s, g] = acc[pl.ds(d, span, stride=dms), :]

    others = (cores - 1) + (xs - 1) + (fft - 1)
    pl.semaphore_wait(barrier, others)

    peer = (core + 1) % cores
    order = list(range(1, fft)) + [0]

    def to_core(s, k):
        xd, g = (x + s) % xs, (f + k) % fft
        return pltpu.make_async_remote_copy(
            part.at[peer, xd, g], r1.at[s, k], s1.at[s, k], v1.at[s, k],
            device_id={"chan": x * cores + peer}, device_id_type=MESH,
        )

    def to_x(s, k):
        return pltpu.make_async_remote_copy(
            q.at[s, k], r2.at[s, k], s2.at[s, k], v2.at[s, k],
            device_id={"chan": ((x + s) % xs) * cores + core}, device_id_type=MESH,
        )

    def to_fft(k):
        return pltpu.make_async_remote_copy(
            total.at[k], r3.at[k], s3.at[k], v3.at[k],
            device_id={"fft": (f + k) % fft}, device_id_type=MESH,
        )

    for k in order:
        for s in list(range(1, xs)) + [0]:
            to_core(s, k).start()
    for k in order:
        for s in range(1, xs):
            to_core(s, k).wait()
            q[s, k] = part[core, (x + s) % xs, (f + k) % fft] + r1[s, k]
            to_x(s, k).start()
    for k in order:
        to_core(0, k).wait()
        value = part[core, x, (f + k) % fft] + r1[0, k]
        for s in range(1, xs):
            to_x(s, k).wait()
            value = value + r2[s, k]
        total[k] = value
        if k:
            to_fft(k).start()

    accel = accel_ref[...]
    bank = bank_ref.shape[1]
    accels = accel.shape[1]
    taps = bank_ref.shape[2]
    chosen = jnp.where(
        lax.broadcasted_iota(jnp.int32, (bank, accels), 0) == accel, 1.0, 0.0
    ).astype(jnp.bfloat16)
    rows = []
    for part_index in range(2):
        row = lax.dot_general(
            chosen, bank_ref[part_index], (((0,), (0,)), ((), ())),
            preferred_element_type=jnp.float32,
        )
        rows.append(jnp.concatenate([row, jnp.zeros((accels, LANES - taps), jnp.float32)], axis=1))
    for kk in range(LANES // 2):
        for part_index in range(2):
            shifted = pltpu.roll(rows[part_index], kk, 1) if kk else rows[part_index]
            tmat[kk * accels:(kk + 1) * accels, part_index * LANES:(part_index + 1) * LANES] = (
                shifted.astype(jnp.bfloat16)
            )

    for k in range(1, fft):
        to_fft(k).wait()
    for z in range(fft):
        own = (f - z + fft) % fft
        def place(z=z, own=own):
            src = r3[own]
            grid_ref[z * blocks:(z + 1) * blocks, :] = src[MAXD:, :]
            if z:
                grid_ref[z * blocks - MAXD:z * blocks, :] += src[:MAXD, :]
        if z == 0:
            r3[0] = total[0]
        place()

    wide = grid_ref.shape[0]
    half = wide // 2
    data = grid_ref[...] if wide == LANES else grid_ref[...].reshape(LANES, wide)
    mixed = jnp.dot(one_ref[...], data, precision=HIGHEST, preferred_element_type=jnp.float32)
    re, im = mixed[:LANES], mixed[LANES:]
    tc, ts = twist_ref[0], twist_ref[1]
    turned = jnp.concatenate([re * tc + im * ts, im * tc - re * ts], axis=1)
    spec = jnp.dot(turned, two_ref[...], precision=HIGHEST, preferred_element_type=jnp.float32)

    lane = lax.broadcasted_iota(jnp.int32, (16, 2 * half), 1)
    low = lax.broadcasted_iota(jnp.int32, (64, 2 * half), 1) < half
    low16 = lane < half
    sides = []
    energy = jnp.float32(0.0)
    square = jnp.zeros((LANES, 2 * half), jnp.float32)
    for part_index in range(2):
        o = spec[:, part_index * 2 * half:(part_index + 1) * 2 * half]
        square = square + o * o
        before = jnp.where(lane == 0, 0.0, pltpu.roll(o[LANES - 16:], 1, 1))
        after = jnp.where(lane == 2 * half - 1, 0.0, pltpu.roll(o[:16], 2 * half - 1, 1))
        sides.append(
            jnp.concatenate(
                [
                    jnp.where(low16, before, o[48:64]),
                    jnp.where(low, o[:64], o[64:]),
                    jnp.where(low16, o[64:80], after),
                    jnp.zeros((32, 2 * half), jnp.float32),
                ],
                axis=0,
            ).astype(jnp.bfloat16)
        )
    energy_ref[0] = jnp.sum(square) * 0.5
    sr, si = sides
    window = jnp.concatenate(
        [jnp.concatenate([sr, si], axis=1), jnp.concatenate([-si, sr], axis=1)], axis=0
    )
    best = jnp.zeros((accels, 2 * half), jnp.float32)
    group = 8
    for g in range(LANES // 2 // group):
        out = jnp.dot(
            tmat[g * group * accels:(g + 1) * group * accels, :], window,
            preferred_element_type=jnp.float32,
        )
        for kk in range(group):
            rr = out[kk * accels:(kk + 1) * accels, :2 * half]
            ii = out[kk * accels:(kk + 1) * accels, 2 * half:]
            best = jnp.maximum(best, rr * rr + ii * ii)
    best = jnp.maximum(best, pltpu.roll(best, half, 1))
    peaks_ref[0] = best[:, :half]


def solution(mesh):
    fft, chan = mesh.shape["fft"], mesh.shape["chan"]
    cores = 2
    xs = chan // cores

    def body(filterbank, delays, template_bank, accel_index):
        channels, samples = filterbank.shape
        dms = delays.shape[1]
        accels = accel_index.shape[0]
        length = samples * fft
        blocks = samples // LANES
        span = blocks + MAXD
        wide = length // LANES
        chunk = 512
        one, twist, two = tables(length, channels * chan)
        f32, bf16 = jnp.float32, jnp.bfloat16
        vmem = pl.BlockSpec(memory_space=pltpu.VMEM)
        dma = pltpu.SemaphoreType.DMA
        return pl.pallas_call(
            functools.partial(kernel, (fft, xs, cores, dms, blocks, chunk)),
            out_shape=(
                jax.ShapeDtypeStruct((1, accels, wide // 2), f32),
                jax.ShapeDtypeStruct((1,), f32),
            ),
            in_specs=[pl.BlockSpec(memory_space=pl.ANY)] + [vmem] * 6,
            out_specs=(vmem, pl.BlockSpec(memory_space=pltpu.SMEM)),
            scratch_shapes=[
                pltpu.VMEM((samples // chunk, channels, chunk), bf16),
                pltpu.VMEM((MAXD * dms, channels), bf16),
                pltpu.VMEM((span * dms, LANES), f32),
                pltpu.VMEM((cores, xs, fft, span, LANES), f32),
                pltpu.VMEM((xs, fft, span, LANES), f32),
                pltpu.VMEM((xs, fft, span, LANES), f32),
                pltpu.VMEM((xs, fft, span, LANES), f32),
                pltpu.VMEM((fft, span, LANES), f32),
                pltpu.VMEM((fft, span, LANES), f32),
                pltpu.VMEM((wide, LANES), f32),
                pltpu.VMEM((LANES // 2 * accels, 2 * LANES), bf16),
                dma((samples // chunk,)),
                dma((xs, fft)), dma((xs, fft)),
                dma((xs, fft)), dma((xs, fft)),
                dma((fft,)), dma((fft,)),
            ],
            compiler_params=pltpu.CompilerParams(
                collective_id=0, has_side_effects=True, vmem_limit_bytes=56 * 2 ** 20
            ),
            name="search",
        )(
            filterbank, delays.T, template_bank, accel_index[None, :], one, twist, two
        )

    in_specs = (P(("beam", "chan"), "fft"), P("chan", None), P(), P())
    out_specs = (P(("beam", "fft", "chan"), None, None), P(("beam", "fft", "chan")))
    return jax.shard_map(body, mesh=mesh, in_specs=in_specs, out_specs=out_specs, check_vma=False)
```

time: 241 us -> 25.6 us (0.11)
  matrix products: 127 us -> 0 us
  waiting for transfers between devices: 41.6 us -> 0 us
  local copies, waits for them, and re-layouts: 41.7 us -> 2.81 us
  Pallas kernels: 0 us -> 20 us
  between operations: 14.8 us -> 2.46 us
  starting transfers between devices: 5.92 us -> 0 us
  loops' own time: 5.59 us -> 0 us
  other arithmetic: 2.68 us -> 0 us
    dot_general x56 -> x0, matrix products: 127 us -> none  [the longest x32 119 us: accumulate(): return running + jnp.dot(picked, window, preferred_element_type=jnp.float32)]
    unnamed x2 -> x0, waiting for transfers between devices: 36 us -> none
    pallas_call x0 -> x1, Pallas kernels: none -> 20 us  [body(): pl.pallas_call(functools.partial(kernel, (fft, xs, cores, dms, blocks, ch...]
    concatenate x2 -> x0, local copies, waits for them, and re-layouts: 15.7 us -> none  [the longest x1 9.16 us: body(): extended = jnp.concatenate([filterbank, blank], axis=1)]
    another operation x40 -> x0, local copies, waits for them, and re-layouts: 11 us -> none  [the longest x24 6.72 us: one_block(): jnp.stack([seg_real[:, lag_index:lag_index + block_bins] for lag_index in...]
    another operation x3 -> x0, loops' own time: 5.59 us -> none  [the longest x1 5.56 us: correlate(): block_peaks = lax.map(one_block, jnp.arange(8, dtype=jnp.int32))]
    all_to_all x1 -> x0, waiting for transfers between devices: 5.54 us -> none  [body(): lax.all_to_all(reduced, 'fft', split_axis=0, concat_axis=1, tiled=True)]
    dynamic_slice x8 -> x0, local copies, waits for them, and re-layouts: 5.15 us -> none  [correlate(): block_peaks = lax.map(one_block, jnp.arange(8, dtype=jnp.int32))]
  transfers between devices with their start and end apart: 3 -> 0, of which waited for: 2 -> 0; matrix products, arithmetic and copies ran while one was open for 35% -> 0% of each run, Pallas kernels for 0% -> 0%
where the time goes in v1:
time: 25.6 us; the launch traced here: 25.3 us
  Pallas kernels  20 us (78%)
  local copies, waits for them, and re-layouts  2.81 us (11%)
  between operations  2.46 us (10%)
    pallas_call x1, Pallas kernels, body(): pl.pallas_call(functools.partial(kernel, (fft, xs, cores, dms, blocks, ch...  20 us
    unnamed x2, local copies, waits for them, and re-layouts  2.81 us

profile of v1, /device:TPU:0, one launch (start us, length us, event | category | flops | bytes accessed | tf_op | source)
XLA Modules:
  0.0 25.3 jit_solution(14818801625896073410)
XLA Ops:
  0.6 1.4 %copy.9.bank_ref = bf16[2,128,32]{2,1,0:T(8,128)(2,1)} copy(bf16[2,128,32]{1,2,0:T(8,128)(2,1)} %param.9) | data formatting | bytes 32768 | tf_op args[2]
  2.1 20.0 %search.1 = (f32[1,64,64]{2,1,0:T(8,128)}, f32[1]{0:T(128)}) custom-call(bf16[1024,4096]{1,0:T(8,128)(2,1)} %fb_ref.1, s32[16,1024]{1,0:T(8,128)} %bitcast.2, bf16[2,128,32]{2,1,0:T(8,128)(2,1)} %copy.9.bank_ref, s32[1,64]{1,0:T(1,128)} %bitcast.3, f32[256,128]{1,0:T(8,128)} %constant.6.clone.one_ref, f32[2,128,128]{2,1,0:T(8,128)} %constant.7.clone.twist_ref, ...), custom_call_target="tpu_custom_call" | custom-call | tf_op jit(solution)/shard_map/search/pallas_call | solution.py:245
  22.1 1.4 %copy.12 = f32[1,64,64]{2,1,0:T(8,128)} copy(f32[1,64,64]{2,1,0:T(8,128)} %get-tuple-element.4) | data formatting | bytes 32768

commit v2 on v1

--- a/solution.py
+++ b/solution.py
@@ -33,12 +33,12 @@
     return [jnp.asarray(t, jnp.float32) for t in (one, twist, two)]
 
 
-def kernel(
+def collect(
     sizes,
-    fb_ref, delay_ref, bank_ref, accel_ref, one_ref, twist_ref, two_ref,
-    peaks_ref, energy_ref,
-    xbuf, picked, acc, part, r1, q, r2, total, r3, grid_ref, tmat,
-    fsem, s1, v1, s2, v2, s3, v3,
+    fb_ref, delay_hbm,
+    grid_ref,
+    delay_ref, xbuf, picked, acc, part, r1, q, r2, total, r3,
+    lsem, fsem, s1, v1, s2, v2, s3, v3,
 ):
     fft, xs, cores, dms, blocks, chunk = sizes
     chan = xs * cores
@@ -55,6 +55,8 @@
             fb_ref.at[:, pl.ds(start, chunk)], xbuf.at[i], fsem.at[i]
         )
 
+    lags = pltpu.make_async_copy(delay_hbm, delay_ref, lsem)
+    lags.start()
     for i in range(chunks):
         fetch(i).start()
 
@@ -70,6 +72,7 @@
     for k in range(1, fft):
         pl.semaphore_signal(barrier, inc=1, device_id={"fft": (f + k) % fft}, device_id_type=MESH)
 
+    lags.wait()
     lag = delay_ref[...]
     for o in range(MAXD):
         picked[(MAXD - 1 - o) * dms:(MAXD - o) * dms, :] = jnp.where(lag == o, 1.0, 0.0).astype(
@@ -139,20 +142,34 @@
         if k:
             to_fft(k).start()
 
+    for k in range(1, fft):
+        to_fft(k).wait()
+    r3[0] = total[0]
+    for z in range(fft):
+        own = (f - z + fft) % fft
+        grid_ref[z * blocks:(z + 1) * blocks, :] = r3[own, MAXD:, :]
+        if z:
+            grid_ref[z * blocks - MAXD:z * blocks, :] += r3[own, :MAXD, :]
+
+
+def search(
+    grid_hbm, bank_ref, accel_ref, one_ref, twist_ref, two_ref, peaks_ref, energy_ref,
+    grid_ref, tmat, gsem,
+):
+    load = pltpu.make_async_copy(grid_hbm, grid_ref, gsem)
+    load.start()
     accel = accel_ref[...]
-    bank = bank_ref.shape[1]
+    bank = bank_ref.shape[2]
     accels = accel.shape[1]
-    taps = bank_ref.shape[2]
+    taps = bank_ref.shape[1]
     chosen = jnp.where(
         lax.broadcasted_iota(jnp.int32, (bank, accels), 0) == accel, 1.0, 0.0
     ).astype(jnp.bfloat16)
     rows = []
     for part_index in range(2):
-        row = lax.dot_general(
-            chosen, bank_ref[part_index], (((0,), (0,)), ((), ())),
-            preferred_element_type=jnp.float32,
-        )
-        rows.append(jnp.concatenate([row, jnp.zeros((accels, LANES - taps), jnp.float32)], axis=1))
+        row = jnp.dot(bank_ref[part_index], chosen, preferred_element_type=jnp.float32)
+        row = jnp.concatenate([row, jnp.zeros((LANES - taps, accels), jnp.float32)], axis=0)
+        rows.append(row.T)
     for kk in range(LANES // 2):
         for part_index in range(2):
             shifted = pltpu.roll(rows[part_index], kk, 1) if kk else rows[part_index]
@@ -160,19 +177,7 @@
                 shifted.astype(jnp.bfloat16)
             )
 
-    for k in range(1, fft):
-        to_fft(k).wait()
-    for z in range(fft):
-        own = (f - z + fft) % fft
-        def place(z=z, own=own):
-            src = r3[own]
-            grid_ref[z * blocks:(z + 1) * blocks, :] = src[MAXD:, :]
-            if z:
-                grid_ref[z * blocks - MAXD:z * blocks, :] += src[:MAXD, :]
-        if z == 0:
-            r3[0] = total[0]
-        place()
-
+    load.wait()
     wide = grid_ref.shape[0]
     half = wide // 2
     data = grid_ref[...] if wide == LANES else grid_ref[...].reshape(LANES, wide)
@@ -242,15 +247,14 @@
         f32, bf16 = jnp.float32, jnp.bfloat16
         vmem = pl.BlockSpec(memory_space=pltpu.VMEM)
         dma = pltpu.SemaphoreType.DMA
-        return pl.pallas_call(
-            functools.partial(kernel, (fft, xs, cores, dms, blocks, chunk)),
-            out_shape=(
-                jax.ShapeDtypeStruct((1, accels, wide // 2), f32),
-                jax.ShapeDtypeStruct((1,), f32),
-            ),
-            in_specs=[pl.BlockSpec(memory_space=pl.ANY)] + [vmem] * 6,
-            out_specs=(vmem, pl.BlockSpec(memory_space=pltpu.SMEM)),
+        hbm = pl.BlockSpec(memory_space=pltpu.HBM)
+        grid = pl.pallas_call(
+            functools.partial(collect, (fft, xs, cores, dms, blocks, chunk)),
+            out_shape=jax.ShapeDtypeStruct((wide, LANES), f32),
+            in_specs=[hbm] * 2,
+            out_specs=vmem,
             scratch_shapes=[
+                pltpu.VMEM((dms, channels), jnp.int32),
                 pltpu.VMEM((samples // chunk, channels, chunk), bf16),
                 pltpu.VMEM((MAXD * dms, channels), bf16),
                 pltpu.VMEM((span * dms, LANES), f32),
@@ -260,8 +264,7 @@
                 pltpu.VMEM((xs, fft, span, LANES), f32),
                 pltpu.VMEM((fft, span, LANES), f32),
                 pltpu.VMEM((fft, span, LANES), f32),
-                pltpu.VMEM((wide, LANES), f32),
-                pltpu.VMEM((LANES // 2 * accels, 2 * LANES), bf16),
+                dma,
                 dma((samples // chunk,)),
                 dma((xs, fft)), dma((xs, fft)),
                 dma((xs, fft)), dma((xs, fft)),
@@ -270,10 +273,24 @@
             compiler_params=pltpu.CompilerParams(
                 collective_id=0, has_side_effects=True, vmem_limit_bytes=56 * 2 ** 20
             ),
+            name="collect",
+        )(filterbank, delays.T)
+        return pl.pallas_call(
+            search,
+            out_shape=(
+                jax.ShapeDtypeStruct((1, accels, wide // 2), f32),
+                jax.ShapeDtypeStruct((1,), f32),
+            ),
+            in_specs=[hbm] + [vmem] * 5,
+            out_specs=(vmem, pl.BlockSpec(memory_space=pltpu.SMEM)),
+            scratch_shapes=[
+                pltpu.VMEM((wide, LANES), f32),
+                pltpu.VMEM((LANES // 2 * accels, 2 * LANES), bf16),
+                dma,
+            ],
+            compiler_params=pltpu.CompilerParams(vmem_limit_bytes=24 * 2 ** 20),
             name="search",
-        )(
-            filterbank, delays.T, template_bank, accel_index[None, :], one, twist, two
-        )
+        )(grid, template_bank.transpose(0, 2, 1), accel_index[None, :], one, twist, two)
 
     in_specs = (P(("beam", "chan"), "fft"), P("chan", None), P(), P())
     out_specs = (P(("beam", "fft", "chan"), None, None), P(("beam", "fft", "chan")))

time: 25.6 us -> 24.2 us (0.945)
  Pallas kernels: 20 us -> 22.4 us
  local copies, waits for them, and re-layouts: 2.81 us -> 0.86 us
  between operations: 2.46 us -> 0.73 us
    pallas_call x1 -> x2, Pallas kernels: 20 us -> 22.4 us  [the longest x1 19.4 us: body(): pl.pallas_call(functools.partial(collect, (fft, xs, cores, dms, blocks, c...]
    unnamed x2 -> x12, local copies, waits for them, and re-layouts: 2.81 us -> 0.86 us
where the time goes in v2:
time: 24.2 us; the launch traced here: 24 us
  Pallas kernels  22.4 us (93%)
  local copies, waits for them, and re-layouts  0.86 us (4%)
  between operations  0.73 us (3%)
    pallas_call x1, Pallas kernels, body(): pl.pallas_call(functools.partial(collect, (fft, xs, cores, dms, blocks, c...  19.4 us
    pallas_call x1, Pallas kernels, body(): pl.pallas_call(search, out_shape=(jax.ShapeDtypeStruct((1, accels, wide /...  3.02 us
    unnamed x12, local copies, waits for them, and re-layouts  0.86 us

profile of v2, /device:TPU:0, one launch (start us, length us, event | category | flops | bytes accessed | tf_op | source)
XLA Modules:
  0.0 24.0 jit_solution(17833946719137968477)
XLA Ops:
  0.6 0.0 copy-start.1
  0.6 0.0 copy-start.2
  0.7 0.0 copy-start.3
  0.7 0.0 copy-start.5
  0.7 0.0 copy-start.4
  0.7 19.4 %collect.1.grid_hbm = f32[128,128]{1,0:T(8,128)} custom-call(bf16[1024,4096]{1,0:T(8,128)(2,1)} %fb_ref.1, s32[16,1024]{1,0:T(8,128)} %bitcast.5), custom_call_target="tpu_custom_call" | custom-call | tf_op jit(solution)/shard_map/collect/pallas_call | solution.py:251
  20.1 0.0 copy-done.1
  20.1 0.0 copy-done.2
  20.1 0.0 copy-done.3
  20.1 0.0 copy-done.5
  20.1 0.0 copy-done.4
  20.1 0.0 copy-start
  20.1 0.8 %copy-done = f32[128,128]{1,0:T(8,128)S(1)} copy-done((f32[128,128]{1,0:T(8,128)S(1)}, f32[128,128]{1,0:T(8,128)}, u32[]{:S(2)}) %copy-start) | copy-done | bytes 65560
  21.0 3.0 %search.1 = (f32[1,64,64]{2,1,0:T(8,128)}, f32[1]{0:T(128)}) custom-call(f32[128,128]{1,0:T(8,128)S(1)} %copy-done, bf16[2,32,128]{2,1,0:T(8,128)(2,1)S(1)} %bitcast.3, s32[1,64]{1,0:T(1,128)S(1)} %bitcast.4, f32[256,128]{1,0:T(8,128)S(1)} %copy-done.3, f32[2,128,128]{2,1,0:T(8,128)S(1)} %copy-done.2, f32[256,256]{1,0:T(8,128)S(1)} %copy-done.1), custom_call_target="tpu_custom_call" | custom-call | tf_op jit(solution)/shard_map/search/pallas_call | solution.py:278
Async XLA Ops:
  0.6 19.5 %copy-start.1 = (f32[256,256]{1,0:T(8,128)S(1)}, f32[256,256]{1,0:T(8,128)}, u32[]{:S(2)}) copy-start(f32[256,256]{1,0:T(8,128)} %constant.8.clone.two_ref) | copy-start | bytes 786436
  0.6 19.5 %copy-start.2 = (f32[2,128,128]{2,1,0:T(8,128)S(1)}, f32[2,128,128]{2,1,0:T(8,128)}, u32[]{:S(2)}) copy-start(f32[2,128,128]{2,1,0:T(8,128)} %constant.7.clone.twist_ref) | copy-start | bytes 393220
  0.7 19.5 %copy-start.3 = (f32[256,128]{1,0:T(8,128)S(1)}, f32[256,128]{1,0:T(8,128)}, u32[]{:S(2)}) copy-start(f32[256,128]{1,0:T(8,128)} %constant.6.clone.one_ref) | copy-start | bytes 393220
  0.7 19.5 %copy-start.5 = (s32[64]{0:T(128)S(1)}, s32[64]{0:T(128)}, u32[]{:S(2)}) copy-start(s32[64]{0:T(128)} %param.10) | copy-start | bytes 772
  0.7 19.5 %copy-start.4 = (bf16[2,128,32]{1,2,0:T(8,128)(2,1)S(1)}, bf16[2,128,32]{1,2,0:T(8,128)(2,1)}, u32[]{:S(2)}) copy-start(bf16[2,128,32]{1,2,0:T(8,128)(2,1)} %param.9) | copy-start | bytes 49156
  20.1 0.8 %copy-start = (f32[128,128]{1,0:T(8,128)S(1)}, f32[128,128]{1,0:T(8,128)}, u32[]{:S(2)}) copy-start(f32[128,128]{1,0:T(8,128)} %collect.1.grid_hbm) | copy-start | bytes 196612

commit v3 on v2

--- a/solution.py
+++ b/solution.py
@@ -57,7 +57,8 @@
 
     lags = pltpu.make_async_copy(delay_hbm, delay_ref, lsem)
     lags.start()
-    for i in range(chunks):
+    ahead = min(2, chunks)
+    for i in range(ahead):
         fetch(i).start()
 
     barrier = pltpu.get_barrier_semaphore()
@@ -82,6 +83,11 @@
 
     def gather_columns(i, carry):
         fetch(i).wait()
+
+        @pl.when(i + ahead < chunks)
+        def _():
+            fetch(i + ahead).start()
+
         for b in range(chunk // 256):
             y = jnp.dot(
                 picked[...], xbuf[i, :, b * 256:(b + 1) * 256], preferred_element_type=jnp.float32
@@ -242,7 +248,7 @@
         blocks = samples // LANES
         span = blocks + MAXD
         wide = length // LANES
-        chunk = 512
+        chunk = 1024
         one, twist, two = tables(length, channels * chan)
         f32, bf16 = jnp.float32, jnp.bfloat16
         vmem = pl.BlockSpec(memory_space=pltpu.VMEM)

time: 24.2 us -> 22.2 us (0.917)
  Pallas kernels: 22.4 us -> 20.5 us
    pallas_call x1, Pallas kernels: 19.4 us -> 17.4 us  [body(): pl.pallas_call(functools.partial(collect, (fft, xs, cores, dms, blocks, c...]
where the time goes in v3:
time: 22.2 us; the launch traced here: 22.1 us
  Pallas kernels  20.5 us (92%)
  local copies, waits for them, and re-layouts  0.86 us (4%)
  between operations  0.73 us (3%)
    pallas_call x1, Pallas kernels, body(): pl.pallas_call(functools.partial(collect, (fft, xs, cores, dms, blocks, c...  17.4 us
    pallas_call x1, Pallas kernels, body(): pl.pallas_call(search, out_shape=(jax.ShapeDtypeStruct((1, accels, wide /...  3.02 us
    unnamed x12, local copies, waits for them, and re-layouts  0.86 us

profile of v3, /device:TPU:0, one launch (start us, length us, event | category | flops | bytes accessed | tf_op | source)
XLA Modules:
  0.0 22.1 jit_solution(13634429064942268330)
XLA Ops:
  0.6 0.0 copy-start.1
  0.6 0.0 copy-start.2
  0.7 0.0 copy-start.3
  0.7 0.0 copy-start.5
  0.7 0.0 copy-start.4
  0.7 17.4 %collect.1.grid_hbm = f32[128,128]{1,0:T(8,128)} custom-call(bf16[1024,4096]{1,0:T(8,128)(2,1)} %fb_ref.1, s32[16,1024]{1,0:T(8,128)} %bitcast.5), custom_call_target="tpu_custom_call" | custom-call | tf_op jit(solution)/shard_map/collect/pallas_call | solution.py:257
  18.1 0.0 copy-done.1
  18.1 0.0 copy-done.2
  18.2 0.0 copy-done.3
  18.2 0.0 copy-done.5
  18.2 0.0 copy-done.4
  18.2 0.0 copy-start
  18.2 0.8 %copy-done = f32[128,128]{1,0:T(8,128)S(1)} copy-done((f32[128,128]{1,0:T(8,128)S(1)}, f32[128,128]{1,0:T(8,128)}, u32[]{:S(2)}) %copy-start) | copy-done | bytes 65560
  19.0 3.0 %search.1 = (f32[1,64,64]{2,1,0:T(8,128)}, f32[1]{0:T(128)}) custom-call(f32[128,128]{1,0:T(8,128)S(1)} %copy-done, bf16[2,32,128]{2,1,0:T(8,128)(2,1)S(1)} %bitcast.3, s32[1,64]{1,0:T(1,128)S(1)} %bitcast.4, f32[256,128]{1,0:T(8,128)S(1)} %copy-done.3, f32[2,128,128]{2,1,0:T(8,128)S(1)} %copy-done.2, f32[256,256]{1,0:T(8,128)S(1)} %copy-done.1), custom_call_target="tpu_custom_call" | custom-call | tf_op jit(solution)/shard_map/search/pallas_call | solution.py:284
Async XLA Ops:
  0.6 17.5 %copy-start.1 = (f32[256,256]{1,0:T(8,128)S(1)}, f32[256,256]{1,0:T(8,128)}, u32[]{:S(2)}) copy-start(f32[256,256]{1,0:T(8,128)} %constant.8.clone.two_ref) | copy-start | bytes 786436
  0.6 17.5 %copy-start.2 = (f32[2,128,128]{2,1,0:T(8,128)S(1)}, f32[2,128,128]{2,1,0:T(8,128)}, u32[]{:S(2)}) copy-start(f32[2,128,128]{2,1,0:T(8,128)} %constant.7.clone.twist_ref) | copy-start | bytes 393220
  0.7 17.5 %copy-start.3 = (f32[256,128]{1,0:T(8,128)S(1)}, f32[256,128]{1,0:T(8,128)}, u32[]{:S(2)}) copy-start(f32[256,128]{1,0:T(8,128)} %constant.6.clone.one_ref) | copy-start | bytes 393220
  0.7 17.5 %copy-start.5 = (s32[64]{0:T(128)S(1)}, s32[64]{0:T(128)}, u32[]{:S(2)}) copy-start(s32[64]{0:T(128)} %param.10) | copy-start | bytes 772
  0.7 17.5 %copy-start.4 = (bf16[2,128,32]{1,2,0:T(8,128)(2,1)S(1)}, bf16[2,128,32]{1,2,0:T(8,128)(2,1)}, u32[]{:S(2)}) copy-start(bf16[2,128,32]{1,2,0:T(8,128)(2,1)} %param.9) | copy-start | bytes 49156
  18.2 0.8 %copy-start = (f32[128,128]{1,0:T(8,128)S(1)}, f32[128,128]{1,0:T(8,128)}, u32[]{:S(2)}) copy-start(f32[128,128]{1,0:T(8,128)} %collect.1.grid_hbm) | copy-start | bytes 196612
